TPU v7x, 256 devices: a whole 4x4x8 slice. The times are simulated.
256 devices in a mesh: ta: 8 (over x, core), xyz: 32 (over y, z).
Axes of the slice: x: 4, y: 4, z: 8, core: 2. Of those that a mesh axis runs over, the one named last changes fastest.
Arguments:
- nulls: bfloat16 [32, 128, 32, 16, 128], P('ta', 'xyz'), may hold values from -1.1953125 to 1.1953125
- time_links: bfloat16 [16, 128, 32, 64, 128], P('ta', 'xyz'), may hold values from -0.5 to 0.5
- space_links: bfloat16 [32, 64, 32, 64, 128], P('ta', 'xyz'), may hold values from -0.5 to 0.5
- owner_lists: int32 [32, 64], replicated, may hold values from -1 to 1023, as said below
Outputs:
- coarse_links: float32 [8, 2048, 1024], P('ta', 'xyz')
Inputs may be any that keep to these rules, and one draw needn't show every extreme that they name: `owner_lists`: row d lists, in increasing order, the aggregates that shard d owns, followed by -1 in the remaining slots; each of the 1024 aggregate ids appears exactly once. Exactly half of the shards own 64 aggregates each and the others none. The 32 aggregates with ids q * 32 to q * 32 + 31 belong to exactly 8 owners, 4 to each.
All inputs are finite; a program needn't handle non-finite values.
Results may differ from a plain program's by a relative error of at most 0.0029.
Values may be sent and summed in bfloat16 or wider, within the bound.
A program may use at most 64 MiB of HBM per device.

v0:
```python
import jax
import jax.numpy as jnp
from jax import lax
from jax.sharding import PartitionSpec as P


def shifted(array, axis, by):
    count = lax.axis_size(axis)
    return lax.ppermute(array, axis, [(i, (i + by) % count) for i in range(count)])


def forward_image(link_mats, upper_nulls):
    half_width = link_mats.shape[-2]
    upper_real = upper_nulls[..., :half_width]
    upper_imag = upper_nulls[..., half_width:]
    paired = jnp.stack(
        [
            jnp.concatenate([upper_real, -upper_imag], axis=-1),
            jnp.concatenate([upper_imag, upper_real], axis=-1),
        ],
        axis=-3,
    )
    image_pair = jnp.einsum(
        "...ik,...pnk->...pni", link_mats, paired, preferred_element_type=jnp.float32
    )
    joined = jnp.concatenate([image_pair[..., 0, :, :], image_pair[..., 1, :, :]], axis=-1)
    return joined.astype(jnp.bfloat16)


def conjugate_pair(lower_nulls):
    half_width = lower_nulls.shape[-1] // 2
    turned = jnp.concatenate(
        [-lower_nulls[..., half_width:], lower_nulls[..., :half_width]], axis=-1
    )
    return jnp.stack([lower_nulls, turned], axis=-3)


def on_device(nulls, time_links, space_links, owner_lists):
    time_rows, space_rows, side_rows, vectors, doubled = nulls.shape
    time_aggs = time_rows // 2
    space_aggs = space_rows // 2
    side_aggs = side_rows // 4
    local_count = time_aggs * space_aggs * side_aggs
    edge_time = shifted(nulls[0:1], "ta", -1)
    upper_time = jnp.concatenate([nulls[2::2], edge_time], axis=0)
    edge_space = shifted(nulls[:, 0:1], "xyz", -1)
    upper_space = jnp.concatenate([nulls[:, 2::2], edge_space], axis=1)
    image_time = forward_image(time_links, upper_time).reshape(
        time_aggs, space_aggs, 2, side_aggs, 4, vectors, doubled
    )
    pair_time = conjugate_pair(nulls[1::2]).reshape(
        time_aggs, space_aggs, 2, side_aggs, 4, 2, vectors, doubled
    )
    block_time = jnp.einsum(
        "txcaypnk,txcaymk->txapnm", pair_time, image_time, preferred_element_type=jnp.float32
    )
    image_space = forward_image(space_links, upper_space).reshape(
        time_aggs, 2, space_aggs, side_aggs, 4, vectors, doubled
    )
    pair_space = conjugate_pair(nulls[:, 1::2]).reshape(
        time_aggs, 2, space_aggs, side_aggs, 4, 2, vectors, doubled
    )
    block_space = jnp.einsum(
        "tcxaypnk,tcxaymk->txapnm", pair_space, image_space, preferred_element_type=jnp.float32
    )
    block_width = 2 * vectors * vectors
    link_rows = jnp.concatenate(
        [
            block_time.reshape(local_count, block_width),
            block_space.reshape(local_count, block_width),
        ],
        axis=1,
    )
    shard_index = lax.axis_index("xyz")
    my_list = lax.dynamic_index_in_dim(owner_lists, shard_index, 0, keepdims=False)
    present = my_list >= 0
    everything = lax.all_gather(link_rows, "xyz", axis=0, tiled=True)
    picked = everything[jnp.maximum(my_list, 0)]
    result = jnp.where(present[:, None], picked, 0.0)
    return result[None]


def solution(mesh):
    return jax.shard_map(
        on_device,
        mesh=mesh,
        in_specs=(
            P("ta", "xyz", None, None, None),
            P("ta", "xyz", None, None, None),
            P("ta", "xyz", None, None, None),
            P(),
        ),
        out_specs=P("ta", "xyz", None),
        check_vma=False,
    )
```

profile of v0, /device:TPU:2, one launch (start us, length us, event | category | flops | bytes accessed | tf_op | source)
XLA Modules:
  0.0 130.2 jit_solution(7621202235726365997)
XLA Ops:
  6.5 1.5 %fusion.37 = (bf16[1,4,32,16,128]{4,3,2,1,0:T(8,128)(2,1)S(1)}, bf16[1,4,32,16,128]{4,3,2,1,0:T(8,128)(2,1)S(1)}) fusion(bf16[4,4,32,16,128]{4,3,2,1,0:T(8,128)(2,1)} %param.4), kind=kLoop, calls=%fused_computation.48 | loop fusion | bytes 2097152 | tf_op jit(solution)/shard_map/slice | solution.py:45
  8.1 0.0 collective-permute-start
  8.1 0.3 copy-done
  8.4 1.2 fusion.39
  9.6 8.3 %collective-permute-start.1 = (bf16[4,1,32,16,128]{4,3,2,1,0:T(8,128)(2,1)}, bf16[4,1,32,16,128]{4,3,2,1,0:T(8,128)(2,1)}, u32[]{:S(2)}, u32[]{:S(2)}) collective-permute-start(bf16[4,1,32,16,128]{4,3,2,1,0:T(8,128)(2,1)} %get-tuple-element.12), channel_id=1, source_target_pairs={{0,31},{1,0},{2,1},{3,2},{4,3},{5,4},{6,5},{7,6},{8,7},{9,8},{10,9... | collective-permute-start | bytes 1572872 | tf_op jit(solution)/shard_map/ppermute | solution.py:9
  17.9 0.2 slice.60
  18.1 0.2 slice.69
  18.3 0.4 slice_negate_fusion.1
  18.7 0.6 pad_maximum_fusion.4
  19.3 0.4 slice_negate_fusion
  19.7 0.6 pad_maximum_fusion.5
  20.3 0.7 fusion.34
  21.1 1.2 maximum_bitcast_fusion
  22.2 1.0 copy-done.1
  23.3 2.3 %fusion.14 = bf16[2,4,32,2,16,64]{5,4,3,2,1,0:T(8,128)(2,1)S(1)} fusion(bf16[2,4,32,64,128]{4,3,2,1,0:T(8,128)(2,1)S(1)} %copy-done.1, bf16[2,4,32,1,16,128]{5,4,3,2,1,0:T(8,128)(2,1)S(1)} %get-tuple-element.14, bf16[2,4,32,1,16,128]{5,4,3,2,1,0:T(8,128)(2,1)S(1)} %get-tuple-element.13), kind=kOutput, calls=%fused_computation.17 | convolution fusion | flops 135790592 | bytes 7340032 | tf_op jit(solution)/shard_map/...ik,...pnk->...pni/dot_general | solution.py:23
  25.5 0.6 fusion.36
  26.1 1.0 fusion.24
  27.1 0.3 reshape.75
  27.4 2.3 %collective-permute-done.1 = bf16[4,1,32,16,128]{4,3,2,1,0:T(8,128)(2,1)} collective-permute-done((bf16[4,1,32,16,128]{4,3,2,1,0:T(8,128)(2,1)}, bf16[4,1,32,16,128]{4,3,2,1,0:T(8,128)(2,1)}, u32[]{:S(2)}, u32[]{:S(2)}) %collective-permute-start.1) | collective-permute-done | bytes 524320 | tf_op jit(solution)/shard_map/ppermute | solution.py:9
  29.7 1.9 %fusion.35 = (bf16[4,2,32,16,64]{4,3,2,1,0:T(8,128)(2,1)S(1)}, bf16[4,2,32,16,64]{4,3,2,1,0:T(8,128)(2,1)S(1)}, bf16[4,2,32,16,64]{4,3,2,1,0:T(8,128)(2,1)S(1)}) fusion(bf16[4,1,32,16,128]{4,3,2,1,0:T(8,128)(2,1)} %collective-permute-done.1, bf16[4,1,32,16,128]{4,3,2,1,0:T(8,128)(2,1)S(1)} %copy-done.3), kind=kLoop, calls=%fused_computation.46 | loop fusion | flops 2621440 | bytes 2621440 | tf_op jit(solution)/shard_map/neg | solution.py:18
  31.7 1.2 maximum_bitcast_fusion.3
  32.8 1.0 copy-done.2
  33.9 2.3 %fusion.19 = bf16[4,2,32,2,16,64]{5,4,3,2,1,0:T(8,128)(2,1)S(1)} fusion(bf16[4,2,32,64,128]{4,3,2,1,0:T(8,128)(2,1)S(1)} %copy-done.2, bf16[4,2,32,1,16,128]{5,4,3,2,1,0:T(8,128)(2,1)S(1)} %get-tuple-element.21, bf16[4,2,32,1,16,128]{5,4,3,2,1,0:T(8,128)(2,1)S(1)} %get-tuple-element.20), kind=kOutput, calls=%fused_computation.18 | convolution fusion | flops 135790592 | bytes 7340032 | tf_op jit(solution)/shard_map/...ik,...pnk->...pni/dot_general | solution.py:23
  36.1 0.6 fusion.38
  36.7 1.0 fusion.27
  37.7 0.3 reshape.76
  38.0 0.7 pad_maximum_fusion.6
  38.7 0.7 maximum_bitcast_fusion.6
  39.4 0.7 compare_bitcast_fusion
  40.1 79.5 %all-gather.2.cloned.1.call-done = f32[1024,1024]{1,0:T(8,128)} async-done(((f32[32,1024]{1,0:T(8,128)}), f32[1024,1024]{1,0:T(8,128)}) %all-gather.2.cloned.1.call-update) | async-done | bytes 4194320 | tf_op jit(solution)/shard_map/all_gather | solution.py:77
  119.6 3.0 %gather_fusion = f32[64,1024]{1,0:T(8,128)S(1)} fusion(f32[1024,1024]{1,0:T(8,128)} %all-gather.2.cloned.1.call-done, s32[1024]{0:T(1024)S(1)} %pad_clamp_fusion), kind=kCustom, calls=%fused_computation | custom fusion | bytes 524544 | tf_op jit(solution)/shard_map/gather | solution.py:78
  122.5 0.8 bitcast_select_fusion
  (9 shorter events, 0.0 us)
Async XLA Ops:
  6.5 1.9 %copy-start = (bf16[4,4,32,16,128]{4,3,2,1,0:T(8,128)(2,1)S(1)}, bf16[4,4,32,16,128]{4,3,2,1,0:T(8,128)(2,1)}, u32[]{:S(2)}) copy-start(bf16[4,4,32,16,128]{4,3,2,1,0:T(8,128)(2,1)} %param.4) | copy-start | bytes 6291460
  6.5 113.0 %all-gather.2.cloned.1.call-start = ((), (), s32[]{:S(2)}) async-start(), calls=%async_computation | async-start | bytes 4325376 | tf_op jit(solution)/shard_map/all_gather | solution.py:77
  8.1 12.3 %collective-permute-start = (bf16[1,4,32,16,128]{4,3,2,1,0:T(8,128)(2,1)S(1)}, bf16[1,4,32,16,128]{4,3,2,1,0:T(8,128)(2,1)S(1)}, u32[]{:S(2)}, u32[]{:S(2)}) collective-permute-start(bf16[1,4,32,16,128]{4,3,2,1,0:T(8,128)(2,1)S(1)} %get-tuple-element.8), channel_id=1, source_target_pairs={{0,224},{32,0},{64,32},{96,64},{128,96},{160,128},{192,160},{224,1... | collective-permute-start | bytes 1572872 | tf_op jit(solution)/shard_map/ppermute | solution.py:9
  9.6 20.1 %collective-permute-start.1 = (bf16[4,1,32,16,128]{4,3,2,1,0:T(8,128)(2,1)}, bf16[4,1,32,16,128]{4,3,2,1,0:T(8,128)(2,1)}, u32[]{:S(2)}, u32[]{:S(2)}) collective-permute-start(bf16[4,1,32,16,128]{4,3,2,1,0:T(8,128)(2,1)} %get-tuple-element.12), channel_id=1, source_target_pairs={{0,31},{1,0},{2,1},{3,2},{4,3},{5,4},{6,5},{7,6},{8,7},{9,8},{10,9... | collective-permute-start | bytes 1572872 | tf_op jit(solution)/shard_map/ppermute | solution.py:9
  21.1 2.2 %copy-start.1 = (bf16[2,4,32,64,128]{4,3,2,1,0:T(8,128)(2,1)S(1)}, bf16[2,4,32,64,128]{4,3,2,1,0:T(8,128)(2,1)}, u32[]{:S(2)}) copy-start(bf16[2,4,32,64,128]{4,3,2,1,0:T(8,128)(2,1)} %param.5) | copy-start | bytes 12582916
  26.1 3.6 %copy-start.3 = (bf16[4,1,32,16,128]{4,3,2,1,0:T(8,128)(2,1)S(1)}, bf16[4,1,32,16,128]{4,3,2,1,0:T(8,128)(2,1)}, u32[]{:S(2)}) copy-start(bf16[4,1,32,16,128]{4,3,2,1,0:T(8,128)(2,1)} %get-tuple-element.11) | copy-start | bytes 1572868
  31.7 2.2 %copy-start.2 = (bf16[4,2,32,64,128]{4,3,2,1,0:T(8,128)(2,1)S(1)}, bf16[4,2,32,64,128]{4,3,2,1,0:T(8,128)(2,1)}, u32[]{:S(2)}) copy-start(bf16[4,2,32,64,128]{4,3,2,1,0:T(8,128)(2,1)} %param.6) | copy-start | bytes 12582916
Sparse Core Ops, SparseCore 0:
  38.8 80.7 all-gather.1
where the time goes:
time: 130 us
  waiting for transfers between devices  81.8 us (63%)
  between operations  13.5 us (10%)
  local copies, waits for them, and re-layouts  10.1 us (8%)
  other arithmetic  9.83 us (8%)
  starting transfers between devices  8.33 us (6%)
  matrix products  6.58 us (5%)
    all_gather x1, waiting for transfers between devices, on_device(): everything = lax.all_gather(link_rows, 'xyz', axis=0, tiled=True)  79.5 us
    ppermute x2, starting transfers between devices, shifted(): lax.ppermute(array, axis, [(i, (i + by) % count) for i in range(count)])  8.32 us
    dot_general x2, matrix products, forward_image(): jnp.einsum('...ik,...pnk->...pni', link_mats, paired, preferred_element_t...  4.55 us
    gather x1, local copies, waits for them, and re-layouts, on_device(): picked = everything[jnp.maximum(my_list, 0)]  2.98 us
    neg x2, other arithmetic, forward_image(): -upper_imag  2.63 us
  transfers between devices with their start and end apart: 3, of which 2 were waited for; matrix products, arithmetic and copies ran while one was open for 8% of the time, Pallas kernels for 0%

commit v1 on v0

--- a/solution.py
+++ b/solution.py
@@ -74,7 +74,9 @@
     shard_index = lax.axis_index("xyz")
     my_list = lax.dynamic_index_in_dim(owner_lists, shard_index, 0, keepdims=False)
     present = my_list >= 0
-    everything = lax.all_gather(link_rows, "xyz", axis=0, tiled=True)
+    everything = jnp.concatenate(
+        lax.all_to_all(jnp.stack([link_rows] * lax.axis_size("xyz")), "xyz", 0, 0), axis=0
+    )
     picked = everything[jnp.maximum(my_list, 0)]
     result = jnp.where(present[:, None], picked, 0.0)
     return result[None]

time: 130 us -> 142 us (1.092)
  waiting for transfers between devices: 81.8 us -> 97.5 us
  between operations: 13.5 us -> 0.17 us
  starting transfers between devices: 8.33 us -> 15.9 us
  local copies, waits for them, and re-layouts: 10.1 us -> 12.4 us
    all_to_all x0 -> x1, waiting for transfers between devices: none -> 95.1 us  [on_device(): lax.all_to_all(jnp.stack([link_rows] * lax.axis_size('xyz')), 'xyz', 0, 0)]
    all_gather x1 -> x0, waiting for transfers between devices: 79.5 us -> none  [on_device(): everything = lax.all_gather(link_rows, 'xyz', axis=0, tiled=True)]
    all_to_all x0 -> x1, starting transfers between devices: none -> 7.59 us  [on_device(): lax.all_to_all(jnp.stack([link_rows] * lax.axis_size('xyz')), 'xyz', 0, 0)]
    another operation x0 -> x1, local copies, waits for them, and re-layouts: none -> 2.51 us  [on_device(): jnp.stack([link_rows] * lax.axis_size('xyz'))]
where the time goes in v1:
time: 142 us
  waiting for transfers between devices  97.5 us (69%)
  starting transfers between devices  15.9 us (11%)
  local copies, waits for them, and re-layouts  12.4 us (9%)
  other arithmetic  9.22 us (6%)
  matrix products  6.58 us (5%)
    all_to_all x1, waiting for transfers between devices, on_device(): lax.all_to_all(jnp.stack([link_rows] * lax.axis_size('xyz')), 'xyz', 0, 0)  95.1 us
    ppermute x2, starting transfers between devices, shifted(): lax.ppermute(array, axis, [(i, (i + by) % count) for i in range(count)])  8.32 us
    all_to_all x1, starting transfers between devices, on_device(): lax.all_to_all(jnp.stack([link_rows] * lax.axis_size('xyz')), 'xyz', 0, 0)  7.59 us
    dot_general x2, matrix products, forward_image(): jnp.einsum('...ik,...pnk->...pni', link_mats, paired, preferred_element_t...  4.55 us
    gather x1, local copies, waits for them, and re-layouts, on_device(): picked = everything[jnp.maximum(my_list, 0)]  2.98 us
  transfers between devices with their start and end apart: 3, of which 2 were waited for; matrix products, arithmetic and copies ran while one was open for 8% of the time, Pallas kernels for 0%

profile of v1, /device:TPU:2, one launch (start us, length us, event | category | flops | bytes accessed | tf_op | source)
XLA Modules:
  0.0 141.7 jit_solution(1060848002997325754)
XLA Ops:
  0.0 1.5 %fusion.37 = (bf16[1,4,32,16,128]{4,3,2,1,0:T(8,128)(2,1)S(1)}, bf16[1,4,32,16,128]{4,3,2,1,0:T(8,128)(2,1)S(1)}) fusion(bf16[4,4,32,16,128]{4,3,2,1,0:T(8,128)(2,1)} %param.4), kind=kLoop, calls=%fused_computation.48 | loop fusion | bytes 2097152 | tf_op jit(solution)/shard_map/slice | solution.py:45
  1.6 0.3 copy-done
  1.9 1.0 fusion.39
  2.9 8.3 %collective-permute-start.1 = (bf16[4,1,32,16,128]{4,3,2,1,0:T(8,128)(2,1)}, bf16[4,1,32,16,128]{4,3,2,1,0:T(8,128)(2,1)}, u32[]{:S(2)}, u32[]{:S(2)}) collective-permute-start(bf16[4,1,32,16,128]{4,3,2,1,0:T(8,128)(2,1)} %get-tuple-element.12), channel_id=1, source_target_pairs={{0,31},{1,0},{2,1},{3,2},{4,3},{5,4},{6,5},{7,6},{8,7},{9,8},{10,9... | collective-permute-start | bytes 1572872 | tf_op jit(solution)/shard_map/ppermute | solution.py:9
  11.2 0.2 slice.60
  11.4 0.2 slice.69
  11.6 0.4 slice_negate_fusion.1
  12.0 0.6 pad_maximum_fusion.4
  12.6 0.4 slice_negate_fusion
  13.0 0.6 pad_maximum_fusion.5
  13.6 0.7 fusion.34
  14.4 1.2 maximum_bitcast_fusion
  15.5 1.0 copy-done.1
  16.5 2.3 %fusion.14 = bf16[2,4,32,2,16,64]{5,4,3,2,1,0:T(8,128)(2,1)S(1)} fusion(bf16[2,4,32,64,128]{4,3,2,1,0:T(8,128)(2,1)S(1)} %copy-done.1, bf16[2,4,32,1,16,128]{5,4,3,2,1,0:T(8,128)(2,1)S(1)} %get-tuple-element.14, bf16[2,4,32,1,16,128]{5,4,3,2,1,0:T(8,128)(2,1)S(1)} %get-tuple-element.13), kind=kOutput, calls=%fused_computation.17 | convolution fusion | flops 135790592 | bytes 7340032 | tf_op jit(solution)/shard_map/...ik,...pnk->...pni/dot_general | solution.py:23
  18.8 0.6 fusion.36
  19.4 1.0 fusion.24
  20.4 0.3 reshape.80
  20.7 2.3 %collective-permute-done.1 = bf16[4,1,32,16,128]{4,3,2,1,0:T(8,128)(2,1)} collective-permute-done((bf16[4,1,32,16,128]{4,3,2,1,0:T(8,128)(2,1)}, bf16[4,1,32,16,128]{4,3,2,1,0:T(8,128)(2,1)}, u32[]{:S(2)}, u32[]{:S(2)}) %collective-permute-start.1) | collective-permute-done | bytes 524320 | tf_op jit(solution)/shard_map/ppermute | solution.py:9
  23.0 2.0 %fusion.35 = (bf16[4,2,32,16,64]{4,3,2,1,0:T(8,128)(2,1)S(1)}, bf16[4,2,32,16,64]{4,3,2,1,0:T(8,128)(2,1)S(1)}, bf16[4,2,32,16,64]{4,3,2,1,0:T(8,128)(2,1)S(1)}) fusion(bf16[4,1,32,16,128]{4,3,2,1,0:T(8,128)(2,1)} %collective-permute-done.1, bf16[4,1,32,16,128]{4,3,2,1,0:T(8,128)(2,1)S(1)} %get-tuple-element.11), kind=kLoop, calls=%fused_computation.46 | loop fusion | flops 2621440 | bytes 2621440 | tf_op jit(solution)/shard_map/neg | solution.py:18
  25.0 1.2 maximum_bitcast_fusion.3
  26.2 1.0 copy-done.2
  27.2 2.3 %fusion.19 = bf16[4,2,32,2,16,64]{5,4,3,2,1,0:T(8,128)(2,1)S(1)} fusion(bf16[4,2,32,64,128]{4,3,2,1,0:T(8,128)(2,1)S(1)} %copy-done.2, bf16[4,2,32,1,16,128]{5,4,3,2,1,0:T(8,128)(2,1)S(1)} %get-tuple-element.21, bf16[4,2,32,1,16,128]{5,4,3,2,1,0:T(8,128)(2,1)S(1)} %get-tuple-element.20), kind=kOutput, calls=%fused_computation.18 | convolution fusion | flops 135790592 | bytes 7340032 | tf_op jit(solution)/shard_map/...ik,...pnk->...pni/dot_general | solution.py:23
  29.5 0.6 fusion.38
  30.0 1.0 fusion.27
  31.1 0.3 reshape.81
  31.3 2.5 %stack.38 = f32[32,32,1024]{2,1,0:T(8,128)} broadcast(f32[32,1024]{1,0:T(8,128)S(1)} %pad_maximum_fusion.6), dimensions={1,2} | broadcast | bytes 4325376 | tf_op jit(solution)/shard_map/stack | solution.py:78
  33.8 7.6 %all-to-all-start = ((f32[32,32,1024]{2,1,0:T(8,128)}), f32[32,32,1024]{2,1,0:T(8,128)}, u32[]{:S(2)}, u32[]{:S(2)}) async-start(f32[32,32,1024]{2,1,0:T(8,128)} %stack.38), calls=%async_computation | async-start | bytes 8388608 | tf_op jit(solution)/shard_map/all_to_all | solution.py:78
  41.5 0.7 maximum_bitcast_fusion.6
  42.1 0.7 compare_bitcast_fusion
  42.8 95.1 %all-to-all-done = f32[32,32,1024]{2,1,0:T(8,128)} async-done(((f32[32,32,1024]{2,1,0:T(8,128)}), f32[32,32,1024]{2,1,0:T(8,128)}, u32[]{:S(2)}, u32[]{:S(2)}) %all-to-all-start) | async-done | bytes 4194336 | tf_op jit(solution)/shard_map/all_to_all | solution.py:78
  138.0 3.0 %gather_fusion = f32[64,1024]{1,0:T(8,128)S(1)} fusion(f32[1024,1024]{1,0:T(8,128)} %bitcast.25, s32[1024]{0:T(1024)S(1)} %pad_clamp_fusion), kind=kCustom, calls=%fused_computation | custom fusion | bytes 524544 | tf_op jit(solution)/shard_map/gather | solution.py:80
  141.0 0.8 bitcast_select_fusion
  (7 shorter events, 0.0 us)
Async XLA Ops:
  0.0 1.9 %copy-start = (bf16[4,4,32,16,128]{4,3,2,1,0:T(8,128)(2,1)S(1)}, bf16[4,4,32,16,128]{4,3,2,1,0:T(8,128)(2,1)}, u32[]{:S(2)}) copy-start(bf16[4,4,32,16,128]{4,3,2,1,0:T(8,128)(2,1)} %param.4) | copy-start | bytes 6291460
  1.5 12.1 %collective-permute-start = (bf16[1,4,32,16,128]{4,3,2,1,0:T(8,128)(2,1)S(1)}, bf16[1,4,32,16,128]{4,3,2,1,0:T(8,128)(2,1)S(1)}, u32[]{:S(2)}, u32[]{:S(2)}) collective-permute-start(bf16[1,4,32,16,128]{4,3,2,1,0:T(8,128)(2,1)S(1)} %get-tuple-element.8), channel_id=1, source_target_pairs={{0,224},{32,0},{64,32},{96,64},{128,96},{160,128},{192,160},{224,1... | collective-permute-start | bytes 1572872 | tf_op jit(solution)/shard_map/ppermute | solution.py:9
  2.9 20.1 %collective-permute-start.1 = (bf16[4,1,32,16,128]{4,3,2,1,0:T(8,128)(2,1)}, bf16[4,1,32,16,128]{4,3,2,1,0:T(8,128)(2,1)}, u32[]{:S(2)}, u32[]{:S(2)}) collective-permute-start(bf16[4,1,32,16,128]{4,3,2,1,0:T(8,128)(2,1)} %get-tuple-element.12), channel_id=1, source_target_pairs={{0,31},{1,0},{2,1},{3,2},{4,3},{5,4},{6,5},{7,6},{8,7},{9,8},{10,9... | collective-permute-start | bytes 1572872 | tf_op jit(solution)/shard_map/ppermute | solution.py:9
  14.3 2.2 %copy-start.1 = (bf16[2,4,32,64,128]{4,3,2,1,0:T(8,128)(2,1)S(1)}, bf16[2,4,32,64,128]{4,3,2,1,0:T(8,128)(2,1)}, u32[]{:S(2)}) copy-start(bf16[2,4,32,64,128]{4,3,2,1,0:T(8,128)(2,1)} %param.5) | copy-start | bytes 12582916
  25.0 2.2 %copy-start.2 = (bf16[4,2,32,64,128]{4,3,2,1,0:T(8,128)(2,1)S(1)}, bf16[4,2,32,64,128]{4,3,2,1,0:T(8,128)(2,1)}, u32[]{:S(2)}) copy-start(bf16[4,2,32,64,128]{4,3,2,1,0:T(8,128)(2,1)} %param.6) | copy-start | bytes 12582916
  33.8 104.1 %all-to-all-start = ((f32[32,32,1024]{2,1,0:T(8,128)}), f32[32,32,1024]{2,1,0:T(8,128)}, u32[]{:S(2)}, u32[]{:S(2)}) async-start(f32[32,32,1024]{2,1,0:T(8,128)} %stack.38), calls=%async_computation | async-start | bytes 8388608 | tf_op jit(solution)/shard_map/all_to_all | solution.py:78
